TPU v7x, 256 devices: a whole 4x4x8 slice. The times are simulated.
256 devices in a mesh: gx: 16 (over z_hi, y, core), gy: 16 (over z_lo, x).
Axes of the slice: x: 4, y: 4, z: 8 (z_hi: 2, z_lo: 4; z = z_hi * 4 + z_lo), core: 2. Of those that a mesh axis runs over, the one named last changes fastest.
Arguments:
- skip_input: bfloat16 [32, 64, 4096], P(None, 'gx', 'gy'), may hold values from -6 to 6
- w_encoder: bfloat16 [64, 864], replicated, may hold values from -0.625 to 0.625
- w_bottom: bfloat16 [128, 1728], P('gx'), may hold values from -0.3125 to 0.3125
- w_middle: bfloat16 [64, 5184], replicated, may hold values from -0.15625 to 0.15625
- w_upper: bfloat16 [32, 2592], replicated, may hold values from -0.21875 to 0.21875
- cotangent: bfloat16 [32, 64, 4096], P(None, 'gx', 'gy'), may hold values from -6 to 6
Outputs:
- features: bfloat16 [32, 64, 4096], P(None, 'gx', 'gy')
- grad_skip: bfloat16 [32, 64, 4096], P(None, 'gx', 'gy')
- grad_encoder: float32 [64, 864], replicated
- grad_bottom: float32 [128, 1728], P('gx')
- grad_middle: float32 [64, 5184], replicated
- grad_upper: float32 [32, 2592], replicated
All inputs are finite; a program needn't handle non-finite values.
Results may differ from a plain program's by a relative error of at most 0.017.
Values may be sent and summed in bfloat16 or wider, within the bound.
No kernel may reach another device: no remote copies, remote signals or barrier semaphores. Data moves between devices by JAX's collectives and lax.ppermute only.
A program may use at most 64 MiB of HBM per device.

v0:
```python
import math
import jax
import jax.numpy as jnp
from jax import lax
from jax.sharding import PartitionSpec as P

Z = 16


def extended_2(cells, sides, width):
    for axis, dim in sides:
        count = lax.axis_size(axis)
        ends = count - 1
        head = lax.slice_in_dim(cells, 0, width, axis=dim)
        tail = lax.slice_in_dim(cells, cells.shape[dim] - width, cells.shape[dim], axis=dim)
        cells = jnp.concatenate(
            [
                lax.ppermute(tail, axis, [(i, (i + 1) % count) for i in range(ends)]),
                cells,
                lax.ppermute(head, axis, [((i + 1) % count, i) for i in range(ends)]),
            ],
            axis=dim,
        )
    return cells


def z_shift(extended, z_step, z_depth):
    length = extended.shape[2]
    padded = jnp.pad(extended, ((0, 0), (0, 0), (1, 1)))
    shifted = padded[:, :, 1 + z_step : 1 + z_step + length]
    z_index = lax.broadcasted_iota(jnp.int32, (1, 1, length), 2) % z_depth + z_step
    inside = (z_index >= 0) & (z_index < z_depth)
    return jnp.where(inside, shifted, jnp.zeros_like(shifted))


def tap_piece(shifted_set, a, b, c, row_count, col_count, z_depth, flipped):
    x_off, y_off, z_off = (2 - a, 2 - b, 2 - c) if flipped else (a, b, c)
    source = shifted_set[z_off]
    tap_slice = source[
        :, x_off : x_off + row_count, y_off * z_depth : (y_off + col_count) * z_depth
    ]
    return tap_slice.reshape(source.shape[0], row_count * col_count * z_depth)


def conv_forward(extended, weight, row_count, col_count, z_depth):
    in_chan = extended.shape[0]
    shifted_set = [z_shift(extended, z_step, z_depth) for z_step in (-1, 0, 1)]
    total_sum = jnp.zeros((weight.shape[0], row_count * col_count * z_depth), jnp.float32)
    for a in range(3):
        for b in range(3):
            for c in range(3):
                tap_number = 9 * a + 3 * b + c
                total_sum = total_sum + jnp.dot(
                    weight[:, tap_number * in_chan : (tap_number + 1) * in_chan],
                    tap_piece(shifted_set, a, b, c, row_count, col_count, z_depth, False),
                    preferred_element_type=jnp.float32,
                )
    return total_sum


def conv_backward(extended, weight, row_count, col_count, z_depth):
    in_chan = weight.shape[1] // 27
    shifted_set = [z_shift(extended, z_step, z_depth) for z_step in (-1, 0, 1)]
    total_sum = jnp.zeros((in_chan, row_count * col_count * z_depth), jnp.float32)
    for a in range(3):
        for b in range(3):
            for c in range(3):
                tap_number = 9 * a + 3 * b + c
                total_sum = total_sum + lax.dot_general(
                    weight[:, tap_number * in_chan : (tap_number + 1) * in_chan],
                    tap_piece(shifted_set, a, b, c, row_count, col_count, z_depth, True),
                    (((0,), (0,)), ((), ())),
                    preferred_element_type=jnp.float32,
                )
    return total_sum


def weight_grad(extended, error_flat, row_count, col_count, z_depth):
    shifted_set = [z_shift(extended, z_step, z_depth) for z_step in (-1, 0, 1)]
    blocks = []
    for a in range(3):
        for b in range(3):
            for c in range(3):
                blocks.append(
                    lax.dot_general(
                        error_flat,
                        tap_piece(shifted_set, a, b, c, row_count, col_count, z_depth, False),
                        (((1,), (1,)), ((), ())),
                        preferred_element_type=jnp.float32,
                    )
                )
    return jnp.concatenate(blocks, axis=1)


def pool_mean(values, z_depth):
    channels, row_count, length = values.shape
    col_count = length // z_depth
    shaped = values.astype(jnp.float32).reshape(
        channels, row_count // 2, 2, col_count // 2, 2, z_depth // 2, 2
    )
    return shaped.mean(axis=(2, 4, 6)).reshape(
        channels, row_count // 2, col_count // 2 * (z_depth // 2)
    )


def block_sum(values, z_depth):
    channels, row_count, length = values.shape
    col_count = length // z_depth
    shaped = values.reshape(channels, row_count // 2, 2, col_count // 2, 2, z_depth // 2, 2)
    return shaped.sum(axis=(2, 4, 6)).reshape(
        channels, row_count // 2, col_count // 2 * (z_depth // 2)
    )


def upsample(values, z_depth):
    channels, row_count, length = values.shape
    col_count = length // z_depth
    shaped = values.reshape(channels, row_count, 1, col_count, 1, z_depth, 1)
    shaped = jnp.broadcast_to(shaped, (channels, row_count, 2, col_count, 2, z_depth, 2))
    return shaped.reshape(channels, 2 * row_count, 4 * col_count * z_depth)


def silu_slope(values):
    s_value = jax.nn.sigmoid(values)
    return s_value * (1.0 + values * (1.0 - s_value))


def spatial_halo(values, z_depth):
    widened = extended_2(values, (("gx", 1),), 1)
    return extended_2(widened, (("gy", 2),), z_depth)


def per_device(skip_input, w_encoder, w_bottom, w_middle, w_upper, cotangent):
    top_chan = skip_input.shape[0]
    rows_fine = skip_input.shape[1]
    cols_fine = skip_input.shape[2] // Z
    rows_mid, cols_mid, depth_mid = (rows_fine // 2, cols_fine // 2, Z // 2)
    rows_low, cols_low, depth_low = (rows_fine // 4, cols_fine // 4, Z // 4)
    cells_fine = rows_fine * cols_fine * Z * lax.axis_size("gx") * lax.axis_size("gy")
    scale_fine = 1.0 / math.sqrt(cells_fine)
    scale_mid = 1.0 / math.sqrt(cells_fine // 8)
    scale_low = 1.0 / math.sqrt(cells_fine // 64)
    pool_top = pool_mean(skip_input, Z).astype(jnp.bfloat16)
    ext_pool = spatial_halo(pool_top, depth_mid)
    pre_one = conv_forward(ext_pool, w_encoder, rows_mid, cols_mid, depth_mid)
    act_one = jax.nn.silu(pre_one).astype(jnp.bfloat16).reshape(-1, rows_mid, cols_mid * depth_mid)
    pool_mid = pool_mean(act_one, depth_mid).astype(jnp.bfloat16)
    col_ext = extended_2(pool_mid, (("gy", 2),), depth_low)
    whole_rows = lax.all_gather(col_ext, "gx", axis=1, tiled=True)
    ext_low = jnp.pad(whole_rows, ((0, 0), (1, 1), (0, 0)))
    rows_all = whole_rows.shape[1]
    pre_two = conv_forward(ext_low, w_bottom, rows_all, cols_low, depth_low)
    act_block = (
        jax.nn.silu(pre_two).astype(jnp.bfloat16).reshape(-1, rows_all, cols_low * depth_low)
    )
    act_two = lax.all_to_all(act_block, "gx", split_axis=1, concat_axis=0, tiled=True)
    cat_mid = jnp.concatenate([upsample(act_two, depth_low), act_one], axis=0)
    ext_mid = spatial_halo(cat_mid, depth_mid)
    pre_three = conv_forward(ext_mid, w_middle, rows_mid, cols_mid, depth_mid)
    act_three = (
        jax.nn.silu(pre_three).astype(jnp.bfloat16).reshape(-1, rows_mid, cols_mid * depth_mid)
    )
    cat_top = jnp.concatenate([upsample(act_three, depth_mid), skip_input], axis=0)
    ext_top = spatial_halo(cat_top, Z)
    pre_four = conv_forward(ext_top, w_upper, rows_fine, cols_fine, Z)
    features = (
        jax.nn.silu(pre_four).astype(jnp.bfloat16).reshape(top_chan, rows_fine, cols_fine * Z)
    )
    err_four = (cotangent.reshape(top_chan, -1).astype(jnp.float32) * silu_slope(pre_four)).astype(
        jnp.bfloat16
    )
    local_upper = weight_grad(ext_top, err_four, rows_fine, cols_fine, Z) * scale_fine
    grad_upper = lax.psum(local_upper, ("gx", "gy"))
    dcat_top = conv_backward(
        spatial_halo(err_four.reshape(top_chan, rows_fine, cols_fine * Z), Z),
        w_upper,
        rows_fine,
        cols_fine,
        Z,
    ).reshape(-1, rows_fine, cols_fine * Z)
    mid_chan = act_three.shape[0]
    err_three = (
        block_sum(dcat_top[:mid_chan], Z).reshape(mid_chan, -1) * silu_slope(pre_three)
    ).astype(jnp.bfloat16)
    local_middle = weight_grad(ext_mid, err_three, rows_mid, cols_mid, depth_mid) * scale_mid
    grad_middle = lax.psum(local_middle, ("gx", "gy"))
    dcat_mid = conv_backward(
        spatial_halo(err_three.reshape(mid_chan, rows_mid, cols_mid * depth_mid), depth_mid),
        w_middle,
        rows_mid,
        cols_mid,
        depth_mid,
    ).reshape(-1, rows_mid, cols_mid * depth_mid)
    low_chan = act_two.shape[0]
    dact_two = block_sum(dcat_mid[:low_chan], depth_mid)
    dact_block = lax.all_to_all(dact_two, "gx", split_axis=0, concat_axis=1, tiled=True)
    block_chan = dact_block.shape[0]
    err_two = (dact_block.reshape(block_chan, -1) * silu_slope(pre_two)).astype(jnp.bfloat16)
    part_bottom = weight_grad(ext_low, err_two, rows_all, cols_low, depth_low)
    err_grid = err_two.reshape(block_chan, rows_all, cols_low * depth_low)
    err_cols = extended_2(err_grid, (("gy", 2),), depth_low)
    err_ext = jnp.pad(err_cols, ((0, 0), (1, 1), (0, 0)))
    partial_sum = conv_backward(err_ext, w_bottom, rows_all, cols_low, depth_low).reshape(
        -1, rows_all, cols_low * depth_low
    )
    dpool_mid = lax.psum_scatter(
        partial_sum.astype(jnp.bfloat16), "gx", scatter_dimension=1, tiled=True
    ).astype(jnp.float32)
    grad_bottom = lax.psum((part_bottom * scale_low).astype(jnp.bfloat16), "gy").astype(jnp.float32)
    dact_one = dcat_mid[low_chan:] + upsample(dpool_mid, depth_low) / 8.0
    err_one = (dact_one.reshape(mid_chan, -1) * silu_slope(pre_one)).astype(jnp.bfloat16)
    local_encoder = weight_grad(ext_pool, err_one, rows_mid, cols_mid, depth_mid) * scale_mid
    grad_encoder = lax.psum(local_encoder, ("gx", "gy"))
    dpool_top = conv_backward(
        spatial_halo(err_one.reshape(mid_chan, rows_mid, cols_mid * depth_mid), depth_mid),
        w_encoder,
        rows_mid,
        cols_mid,
        depth_mid,
    ).reshape(-1, rows_mid, cols_mid * depth_mid)
    grad_skip = (dcat_top[mid_chan:] + upsample(dpool_top, depth_mid) / 8.0).astype(jnp.bfloat16)
    return (features, grad_skip, grad_encoder, grad_bottom, grad_middle, grad_upper)


def solution(mesh):
    in_specs = (P(None, "gx", "gy"), P(), P("gx", None), P(), P(), P(None, "gx", "gy"))
    out_specs = (P(None, "gx", "gy"), P(None, "gx", "gy"), P(), P("gx", None), P(), P())
    return jax.shard_map(
        per_device, mesh=mesh, in_specs=in_specs, out_specs=out_specs, check_vma=False
    )
```

profile of v0, /device:TPU:4, one launch (start us, length us, event | category | flops | bytes accessed | tf_op | source)
XLA Modules:
  0.0 701.9 jit_solution(12189707919216640930)
XLA Ops:
  8.6 1.7 collective-permute-start
  10.4 1.3 collective-permute-start.1
  12.8 2.0 collective-permute-done.1
  14.8 3.1 collective-permute-start.2
  17.9 2.7 collective-permute-start.3
  21.4 2.1 collective-permute-done.3
  34.1 5.8 collective-permute-start.4
  40.0 1.9 collective-permute-start.5
  41.9 3.5 collective-permute-done.5
  45.4 33.5 %all_gather.3 = bf16[64,16,24]{0,2,1:T(8,128)(2,1)S(1)} all-gather(bf16[64,1,24]{0,2,1:T(8,128)(2,1)S(1)} %pad_maximum_fusion.21), channel_id=1, replica_groups=mesh['gx'=16,'gy'=16] {'gx'}, dimensions={1}, use_global_device_ids=true | all-gather | bytes 52224 | tf_op jit(solution)/shard_map/all_gather | solution.py:149
  86.0 6.4 all-to-all-start
  92.6 9.9 %all-to-all-done = bf16[8,16,16]{2,0,1:T(8,128)(2,1)S(1)} async-done(((bf16[8,16,16]{2,0,1:T(8,128)(2,1)}), bf16[8,16,16]{2,0,1:T(8,128)(2,1)S(1)}, u32[]{:S(2)}, u32[]{:S(2)}) %all-to-all-start) | async-done | bytes 4128 | tf_op jit(solution)/shard_map/all_to_all | solution.py:156
  102.8 2.0 collective-permute-start.6
  104.8 1.3 collective-permute-start.7
  106.2 1.9 collective-permute-done.7
  108.0 4.2 collective-permute-start.8
  112.2 1.9 collective-permute-start.9
  114.2 3.7 collective-permute-done.9
  119.8 1.3 copy-done.1
  127.1 3.1 collective-permute-start.10
  130.2 1.3 collective-permute-start.11
  131.5 2.7 collective-permute-done.11
  134.4 4.1 collective-permute-start.12
  138.4 2.1 collective-permute-start.13
  140.6 3.6 collective-permute-done.13
  157.6 3.4 collective-permute-start.14
  161.1 1.3 collective-permute-start.15
  162.8 2.3 collective-permute-done.15
  165.3 4.1 collective-permute-start.16
  169.3 1.9 collective-permute-start.17
  172.7 2.8 collective-permute-done.17
  188.3 1.7 fusion.424
  190.7 1.6 fusion.422
  209.4 3.1 collective-permute-start.18
  212.5 1.5 collective-permute-start.19
  214.8 2.0 collective-permute-done.19
  217.7 4.0 collective-permute-start.20
  221.7 1.9 collective-permute-start.21
  223.8 1.7 concatenate.78
  225.4 2.7 collective-permute-done.21
  228.2 1.2 broadcast_select_fusion.5
  231.1 1.4 reshape.1182
  232.5 1.4 reshape.1179
  234.0 1.4 reshape.1176
  235.4 1.4 reshape.1173
  241.3 1.4 reshape.1181
  242.7 1.4 reshape.1178
  244.2 1.4 reshape.1175
  245.6 1.4 reshape.1172
  251.4 1.5 reshape.1180
  252.9 1.4 reshape.1177
  270.0 28.7 %all-to-all-start.1 = ((f32[16,1,128]{2,1,0:T(1,128)}), f32[16,1,128]{2,1,0:T(1,128)S(1)}, u32[]{:S(2)}, u32[]{:S(2)}) async-start(f32[16,1,128]{2,1,0:T(1,128)} %reshape.1246), calls=%async_computation.1 | async-start | bytes 16384 | tf_op jit(solution)/shard_map/all_to_all | solution.py:196
  300.3 8.3 %all-to-all-done.1 = f32[16,1,128]{2,1,0:T(1,128)S(1)} async-done(((f32[16,1,128]{2,1,0:T(1,128)}), f32[16,1,128]{2,1,0:T(1,128)S(1)}, u32[]{:S(2)}, u32[]{:S(2)}) %all-to-all-start.1) | async-done | bytes 8224 | tf_op jit(solution)/shard_map/all_to_all | solution.py:196
  314.0 4.3 collective-permute-start.22
  318.3 1.9 collective-permute-start.23
  320.5 3.6 collective-permute-done.23
  335.1 70.2 %psum.29 = bf16[8,1728]{1,0:T(8,128)(2,1)S(1)} all-reduce(bf16[8,1728]{1,0:T(8,128)(2,1)S(1)} %multiply_convert_fusion.3), channel_id=1, replica_groups=mesh['gx'=16,'gy'=16] {'gy'}, use_global_device_ids=true, to_apply=%region_6.7 | all-reduce | flops 13824 | bytes 55296 | tf_op jit(solution)/shard_map/psum | solution.py:209
  407.8 1.3 collective-permute-start.24
  409.1 1.3 collective-permute-start.25
  414.2 1.9 collective-permute-start.26
  416.1 4.2 collective-permute-start.27
  435.2 254.7 %all-reduce.13.cloned.1.call-done = (f32[64,864]{0,1:T(8,128)}, f32[64,5184]{1,0:T(8,128)}, f32[32,2592]{1,0:T(8,128)}) async-done(((f32[64,864]{0,1:T(8,128)}, f32[64,5184]{1,0:T(8,128)}, f32[32,2592]{1,0:T(8,128)}), (f32[64,864]{0,1:T(8,128)}, f32[64,5184]{1,0:T(8,128)}, f32[32,2592]{1,0:T(8,128)})) %all-reduce.13.cloned.1.call-update) | async-done | bytes 1880080 | tf_op jit(solution)/shard_map/psum | solution.py:213
  689.9 1.9 copy.98
  691.8 2.5 copy.159
  (970 shorter events, 140.2 us)
Async XLA Ops:
  8.6 4.2 collective-permute-start
  10.4 4.4 collective-permute-start.1
  12.2 66.9 %copy-start.164 = (pred[24]{0:T(512)(128)(4,1)}, pred[24]{0:T(512)(128)(4,1)S(1)}, u32[]{:S(2)}) copy-start(pred[24]{0:T(512)(128)(4,1)S(1)} %get-tuple-element.326) | copy-start | bytes 76
  12.2 66.9 %copy-start.166 = (pred[24]{0:T(512)(128)(4,1)}, pred[24]{0:T(512)(128)(4,1)S(1)}, u32[]{:S(2)}) copy-start(pred[24]{0:T(512)(128)(4,1)S(1)} %get-tuple-element.327) | copy-start | bytes 76
  14.8 8.8 %collective-permute-start.2 = (bf16[32,4,8]{0,2,1:T(8,128)(2,1)S(1)}, bf16[32,4,8]{0,2,1:T(8,128)(2,1)S(1)}, u32[]{:S(2)}, u32[]{:S(2)}) collective-permute-start(bf16[32,4,8]{0,2,1:T(8,128)(2,1)S(1)} %get-tuple-element.241), channel_id=1, source_target_pairs={{0,1},{1,2},{2,3},{3,4},{4,5},{5,6},{6,7},{7,8},{8,9},{9,10},{10,1... | collective-permute-start | bytes 6152 | tf_op jit(solution)/shard_map/ppermute | solution.py:18
  17.9 5.5 collective-permute-start.3
  34.1 7.8 %collective-permute-start.4 = (bf16[64,1,4]{0,2,1:T(4,128)(2,1)S(1)}, bf16[64,1,4]{0,2,1:T(4,128)(2,1)S(1)}, u32[]{:S(2)}, u32[]{:S(2)}) collective-permute-start(bf16[64,1,4]{0,2,1:T(4,128)(2,1)S(1)} %get-tuple-element.309), channel_id=1, source_target_pairs={{0,1},{1,2},{2,3},{3,4},{4,5},{5,6},{6,7},{7,8},{8,9},{9,10},{10,1... | collective-permute-start | bytes 1544 | tf_op jit(solution)/shard_map/ppermute | solution.py:18
  40.0 5.5 collective-permute-start.5
  41.9 37.3 %copy-start.168 = (pred[24]{0:T(512)(128)(4,1)}, pred[24]{0:T(512)(128)(4,1)S(1)}, u32[]{:S(2)}) copy-start(pred[24]{0:T(512)(128)(4,1)S(1)} %compare_and_fusion.2) | copy-start | bytes 76
  86.0 16.4 %all-to-all-start = ((bf16[8,16,16]{2,0,1:T(8,128)(2,1)}), bf16[8,16,16]{2,0,1:T(8,128)(2,1)S(1)}, u32[]{:S(2)}, u32[]{:S(2)}) async-start(bf16[8,16,16]{2,0,1:T(8,128)(2,1)} %copy.83), calls=%async_computation | async-start | bytes 65536 | tf_op jit(solution)/shard_map/all_to_all | solution.py:156
  102.8 3.3 collective-permute-start.6
  104.8 3.2 collective-permute-start.7
  108.0 6.1 collective-permute-start.8
  112.2 5.6 collective-permute-start.9
  119.8 24.6 %copy-start.83 = (bf16[192,2,64]{0,2,1:T(8,128)(2,1)}, bf16[192,2,64]{0,2,1:T(8,128)(2,1)S(1)}, u32[]{:S(2)}) copy-start(bf16[192,2,64]{0,2,1:T(8,128)(2,1)S(1)} %get-tuple-element.127) | copy-start | bytes 147460
  127.1 4.5 collective-permute-start.10
  130.2 4.1 collective-permute-start.11
  134.4 6.2 collective-permute-start.12
  138.4 5.7 collective-permute-start.13
  157.6 5.1 collective-permute-start.14
  161.1 4.0 collective-permute-start.15
  165.3 7.4 %collective-permute-start.16 = (bf16[32,6,16]{2,1,0:T(8,128)(2,1)S(1)}, bf16[32,6,16]{2,1,0:T(8,128)(2,1)S(1)}, u32[]{:S(2)}, u32[]{:S(2)}) collective-permute-start(bf16[32,6,16]{2,1,0:T(8,128)(2,1)S(1)} %get-tuple-element.138), channel_id=1, source_target_pairs={{0,1},{1,2},{2,3},{3,4},{4,5},{5,6},{6,7},{7,8},{8,9},{9,10},{10,1... | collective-permute-start | bytes 18440 | tf_op jit(solution)/shard_map/ppermute | solution.py:18
  169.3 6.2 collective-permute-start.17
  209.4 5.4 collective-permute-start.18
  212.5 4.3 collective-permute-start.19
  217.7 7.8 %collective-permute-start.20 = (bf16[64,4,8]{2,1,0:T(4,128)(2,1)}, bf16[64,4,8]{2,1,0:T(4,128)(2,1)}, u32[]{:S(2)}, u32[]{:S(2)}) collective-permute-start(bf16[64,4,8]{2,1,0:T(4,128)(2,1)} %get-tuple-element.235), channel_id=1, source_target_pairs={{0,1},{1,2},{2,3},{3,4},{4,5},{5,6},{6,7},{7,8},{8,9},{9,10},{10,1... | collective-permute-start | bytes 12296 | tf_op jit(solution)/shard_map/ppermute | solution.py:18
  221.7 6.5 collective-permute-start.21
  267.9 30.9 %copy-start.86 = (f32[192,128]{1,0:T(8,128)}, f32[192,128]{1,0:T(8,128)S(1)}, u32[]{:S(2)}) copy-start(f32[192,128]{1,0:T(8,128)S(1)} %fusion.22) | copy-start | bytes 294916
  270.0 38.6 %all-to-all-start.1 = ((f32[16,1,128]{2,1,0:T(1,128)}), f32[16,1,128]{2,1,0:T(1,128)S(1)}, u32[]{:S(2)}, u32[]{:S(2)}) async-start(f32[16,1,128]{2,1,0:T(1,128)} %reshape.1246), calls=%async_computation.1 | async-start | bytes 16384 | tf_op jit(solution)/shard_map/all_to_all | solution.py:196
  298.8 107.2 %reduce-scatter.2.cloned.1.call-start = ((), (), s32[]{:S(2)}) async-start(), calls=%async_computation.3 | async-start | bytes 69632 | tf_op jit(solution)/shard_map/reduce_scatter | solution.py:206
  314.0 6.5 collective-permute-start.22
  318.3 5.8 collective-permute-start.23
  330.2 76.5 %copy-start.160 = (f32[64,128]{1,0:T(8,128)S(1)}, f32[64,128]{1,0:T(8,128)}, u32[]{:S(2)}) copy-start(f32[64,128]{1,0:T(8,128)} %get-tuple-element.312) | copy-start | bytes 98308
  330.9 79.4 %copy-start.116 = (bf16[32,128]{1,0:T(8,128)(2,1)S(1)}, bf16[32,128]{1,0:T(8,128)(2,1)}, u32[]{:S(2)}) copy-start(bf16[32,128]{1,0:T(8,128)(2,1)} %copy-done.115) | copy-start | bytes 24580
  330.9 79.6 %copy-start.138 = (bf16[32,128]{1,0:T(8,128)(2,1)S(1)}, bf16[32,128]{1,0:T(8,128)(2,1)}, u32[]{:S(2)}) copy-start(bf16[32,128]{1,0:T(8,128)(2,1)} %copy-done.137) | copy-start | bytes 24580
  331.1 79.5 %copy-start.142 = (bf16[32,128]{1,0:T(8,128)(2,1)S(1)}, bf16[32,128]{1,0:T(8,128)(2,1)}, u32[]{:S(2)}) copy-start(bf16[32,128]{1,0:T(8,128)(2,1)} %copy-done.141) | copy-start | bytes 24580
  331.2 79.6 %copy-start.112 = (bf16[32,128]{1,0:T(8,128)(2,1)S(1)}, bf16[32,128]{1,0:T(8,128)(2,1)}, u32[]{:S(2)}) copy-start(bf16[32,128]{1,0:T(8,128)(2,1)} %copy-done.111) | copy-start | bytes 24580
  331.2 79.7 %copy-start.132 = (bf16[32,128]{1,0:T(8,128)(2,1)S(1)}, bf16[32,128]{1,0:T(8,128)(2,1)}, u32[]{:S(2)}) copy-start(bf16[32,128]{1,0:T(8,128)(2,1)} %copy-done.131) | copy-start | bytes 24580
  331.2 79.9 %copy-start.140 = (bf16[32,128]{1,0:T(8,128)(2,1)S(1)}, bf16[32,128]{1,0:T(8,128)(2,1)}, u32[]{:S(2)}) copy-start(bf16[32,128]{1,0:T(8,128)(2,1)} %copy-done.139) | copy-start | bytes 24580
  331.5 79.7 %copy-start.108 = (bf16[32,128]{1,0:T(8,128)(2,1)S(1)}, bf16[32,128]{1,0:T(8,128)(2,1)}, u32[]{:S(2)}) copy-start(bf16[32,128]{1,0:T(8,128)(2,1)} %copy-done.107) | copy-start | bytes 24580
  331.5 79.9 %copy-start.124 = (bf16[32,128]{1,0:T(8,128)(2,1)S(1)}, bf16[32,128]{1,0:T(8,128)(2,1)}, u32[]{:S(2)}) copy-start(bf16[32,128]{1,0:T(8,128)(2,1)} %copy-done.123) | copy-start | bytes 24580
  331.5 80.0 %copy-start.136 = (bf16[32,128]{1,0:T(8,128)(2,1)S(1)}, bf16[32,128]{1,0:T(8,128)(2,1)}, u32[]{:S(2)}) copy-start(bf16[32,128]{1,0:T(8,128)(2,1)} %copy-done.135) | copy-start | bytes 24580
  331.7 79.9 %copy-start.104 = (bf16[32,128]{1,0:T(8,128)(2,1)S(1)}, bf16[32,128]{1,0:T(8,128)(2,1)}, u32[]{:S(2)}) copy-start(bf16[32,128]{1,0:T(8,128)(2,1)} %copy-done.103) | copy-start | bytes 24580
  331.7 80.0 %copy-start.120 = (bf16[32,128]{1,0:T(8,128)(2,1)S(1)}, bf16[32,128]{1,0:T(8,128)(2,1)}, u32[]{:S(2)}) copy-start(bf16[32,128]{1,0:T(8,128)(2,1)} %copy-done.119) | copy-start | bytes 24580
  331.7 80.2 %copy-start.134 = (bf16[32,128]{1,0:T(8,128)(2,1)S(1)}, bf16[32,128]{1,0:T(8,128)(2,1)}, u32[]{:S(2)}) copy-start(bf16[32,128]{1,0:T(8,128)(2,1)} %copy-done.133) | copy-start | bytes 24580
  332.0 80.0 %copy-start.102 = (bf16[32,128]{1,0:T(8,128)(2,1)S(1)}, bf16[32,128]{1,0:T(8,128)(2,1)}, u32[]{:S(2)}) copy-start(bf16[32,128]{1,0:T(8,128)(2,1)} %copy-done.101) | copy-start | bytes 24580
  332.0 80.1 %copy-start.118 = (bf16[32,128]{1,0:T(8,128)(2,1)S(1)}, bf16[32,128]{1,0:T(8,128)(2,1)}, u32[]{:S(2)}) copy-start(bf16[32,128]{1,0:T(8,128)(2,1)} %copy-done.117) | copy-start | bytes 24580
  332.0 80.3 %copy-start.130 = (bf16[32,128]{1,0:T(8,128)(2,1)S(1)}, bf16[32,128]{1,0:T(8,128)(2,1)}, u32[]{:S(2)}) copy-start(bf16[32,128]{1,0:T(8,128)(2,1)} %copy-done.129) | copy-start | bytes 24580
  332.0 80.4 %copy-start.100 = (bf16[32,128]{1,0:T(8,128)(2,1)S(1)}, bf16[32,128]{1,0:T(8,128)(2,1)}, u32[]{:S(2)}) copy-start(bf16[32,128]{1,0:T(8,128)(2,1)} %copy-done.99) | copy-start | bytes 24580
  332.2 80.3 %copy-start.114 = (bf16[32,128]{1,0:T(8,128)(2,1)S(1)}, bf16[32,128]{1,0:T(8,128)(2,1)}, u32[]{:S(2)}) copy-start(bf16[32,128]{1,0:T(8,128)(2,1)} %copy-done.113) | copy-start | bytes 24580
  332.2 80.4 %copy-start.128 = (bf16[32,128]{1,0:T(8,128)(2,1)S(1)}, bf16[32,128]{1,0:T(8,128)(2,1)}, u32[]{:S(2)}) copy-start(bf16[32,128]{1,0:T(8,128)(2,1)} %copy-done.127) | copy-start | bytes 24580
  332.3 80.6 %copy-start.98 = (bf16[32,128]{1,0:T(8,128)(2,1)S(1)}, bf16[32,128]{1,0:T(8,128)(2,1)}, u32[]{:S(2)}) copy-start(bf16[32,128]{1,0:T(8,128)(2,1)} %copy-done.97) | copy-start | bytes 24580
  332.5 80.4 %copy-start.110 = (bf16[32,128]{1,0:T(8,128)(2,1)S(1)}, bf16[32,128]{1,0:T(8,128)(2,1)}, u32[]{:S(2)}) copy-start(bf16[32,128]{1,0:T(8,128)(2,1)} %copy-done.109) | copy-start | bytes 24580
  332.6 80.6 %copy-start.126 = (bf16[32,128]{1,0:T(8,128)(2,1)S(1)}, bf16[32,128]{1,0:T(8,128)(2,1)}, u32[]{:S(2)}) copy-start(bf16[32,128]{1,0:T(8,128)(2,1)} %copy-done.125) | copy-start | bytes 24580
  332.6 80.7 %copy-start.96 = (bf16[32,128]{1,0:T(8,128)(2,1)S(1)}, bf16[32,128]{1,0:T(8,128)(2,1)}, u32[]{:S(2)}) copy-start(bf16[32,128]{1,0:T(8,128)(2,1)} %copy-done.95) | copy-start | bytes 24580
  332.8 80.6 %copy-start.106 = (bf16[32,128]{1,0:T(8,128)(2,1)S(1)}, bf16[32,128]{1,0:T(8,128)(2,1)}, u32[]{:S(2)}) copy-start(bf16[32,128]{1,0:T(8,128)(2,1)} %copy-done.105) | copy-start | bytes 24580
  332.8 80.7 %copy-start.122 = (bf16[32,128]{1,0:T(8,128)(2,1)S(1)}, bf16[32,128]{1,0:T(8,128)(2,1)}, u32[]{:S(2)}) copy-start(bf16[32,128]{1,0:T(8,128)(2,1)} %copy-done.121) | copy-start | bytes 24580
  332.8 80.9 %copy-start.94 = (bf16[32,128]{1,0:T(8,128)(2,1)S(1)}, bf16[32,128]{1,0:T(8,128)(2,1)}, u32[]{:S(2)}) copy-start(bf16[32,128]{1,0:T(8,128)(2,1)} %copy-done.93) | copy-start | bytes 24580
  332.8 81.0 %copy-start.162 = (bf16[32,128]{1,0:T(8,128)(2,1)S(1)}, bf16[32,128]{1,0:T(8,128)(2,1)}, u32[]{:S(2)}) copy-start(bf16[32,128]{1,0:T(8,128)(2,1)} %copy-done.161) | copy-start | bytes 24580
  335.0 354.9 %all-reduce.13.cloned.1.call-start = ((), (), s32[]{:S(2)}) async-start(), calls=%async_computation.4 | async-start | bytes 4259840 | tf_op jit(solution)/shard_map/psum | solution.py:213
  407.8 6.2 collective-permute-start.24
  409.1 4.9 collective-permute-start.25
  414.2 7.0 collective-permute-start.26
  416.1 6.2 collective-permute-start.27
  (144 other events, 1254.4 us)
Sparse Core Ops, SparseCore 0:
  335.1 68.1 reduce-scatter.1
  421.3 268.5 all-reduce.12
where the time goes:
time: 705 us; the launch traced here: 702 us
  waiting for transfers between devices  307 us (44%)
  starting transfers between devices  108 us (15%)
  blocking collectives  104 us (15%)
  matrix products  87.8 us (12%)
  local copies, waits for them, and re-layouts  58.3 us (8%)
  other arithmetic  19.2 us (3%)
  between operations  17.9 us (3%)
    psum x1, waiting for transfers between devices, per_device(): grad_encoder = lax.psum(local_encoder, ('gx', 'gy'))  255 us
    psum x1, blocking collectives, per_device(): lax.psum((part_bottom * scale_low).astype(jnp.bfloat16), 'gy')  70.2 us
    ppermute x14, starting transfers between devices, extended_2(): lax.ppermute(tail, axis, [(i, (i + 1) % count) for i in range(ends)])  46.2 us
    ppermute x14, waiting for transfers between devices, extended_2(): lax.ppermute(head, axis, [((i + 1) % count, i) for i in range(ends)])  34.1 us
    all_gather x1, blocking collectives, per_device(): whole_rows = lax.all_gather(col_ext, 'gx', axis=1, tiled=True)  33.5 us
    dot_general x108, matrix products, weight_grad(): lax.dot_general(error_flat, tap_piece(shifted_set, a, b, c, row_count, co...  33.3 us
    dot_general x108, matrix products, conv_backward(): lax.dot_general(weight[:, tap_number * in_chan:(tap_number + 1) * in_chan...  32.1 us
    reshape x108, local copies, waits for them, and re-layouts, tap_piece(): return tap_slice.reshape(source.shape[0], row_count * col_count * z_depth)  30.8 us
  transfers between devices with their start and end apart: 32, of which 16 were waited for; matrix products, arithmetic and copies ran while one was open for 4% of the time, Pallas kernels for 0%

commit v1 on v0

--- a/solution.py
+++ b/solution.py
@@ -210,7 +210,7 @@
     dact_one = dcat_mid[low_chan:] + upsample(dpool_mid, depth_low) / 8.0
     err_one = (dact_one.reshape(mid_chan, -1) * silu_slope(pre_one)).astype(jnp.bfloat16)
     local_encoder = weight_grad(ext_pool, err_one, rows_mid, cols_mid, depth_mid) * scale_mid
-    grad_encoder = lax.psum(local_encoder, ("gx", "gy"))
+    grad_encoder = lax.psum(lax.psum(local_encoder, "gy"), "gx")
     dpool_top = conv_backward(
         spatial_halo(err_one.reshape(mid_chan, rows_mid, cols_mid * depth_mid), depth_mid),
         w_encoder,

time: 705 us -> 1000 us (1.42)
  waiting for transfers between devices: 307 us -> 612 us
  local copies, waits for them, and re-layouts: 58.3 us -> 47.7 us
    psum x1 -> x3, waiting for transfers between devices: 255 us -> 489 us  [the longest x1 266 us: per_device(): grad_middle = lax.psum(local_middle, ('gx', 'gy'))]
    reduce_scatter x1, waiting for transfers between devices: 0.01 us -> 67.3 us  [per_device(): lax.psum_scatter(partial_sum.astype(jnp.bfloat16), 'gx', scatter_dimensio...]
    reshape x108, local copies, waits for them, and re-layouts: 30.8 us -> 20.8 us  [tap_piece(): return tap_slice.reshape(source.shape[0], row_count * col_count * z_depth)]
  transfers between devices with their start and end apart: 32 -> 34, of which waited for: 16 -> 19; matrix products, arithmetic and copies ran while one was open for 4% -> 3% of each run, Pallas kernels for 0% -> 0%
where the time goes in v1:
time: 1000 us
  waiting for transfers between devices  612 us (61%)
  starting transfers between devices  110 us (11%)
  blocking collectives  108 us (11%)
  matrix products  94 us (9%)
  local copies, waits for them, and re-layouts  47.7 us (5%)
  between operations  17.3 us (2%)
  other arithmetic  11.3 us (1%)
    psum x1, waiting for transfers between devices, per_device(): grad_middle = lax.psum(local_middle, ('gx', 'gy'))  266 us
    psum x2, waiting for transfers between devices, per_device(): grad_encoder = lax.psum(lax.psum(local_encoder, 'gy'), 'gx')  223 us
    psum x1, blocking collectives, per_device(): lax.psum((part_bottom * scale_low).astype(jnp.bfloat16), 'gy')  74.4 us
    reduce_scatter x1, waiting for transfers between devices, per_device(): lax.psum_scatter(partial_sum.astype(jnp.bfloat16), 'gx', scatter_dimensio...  67.3 us
    ppermute x14, starting transfers between devices, extended_2(): lax.ppermute(tail, axis, [(i, (i + 1) % count) for i in range(ends)])  46.2 us
    dot_general x108, matrix products, weight_grad(): lax.dot_general(error_flat, tap_piece(shifted_set, a, b, c, row_count, co...  40.2 us
    ppermute x14, waiting for transfers between devices, extended_2(): lax.ppermute(head, axis, [((i + 1) % count, i) for i in range(ends)])  36.6 us
    all_gather x1, blocking collectives, per_device(): whole_rows = lax.all_gather(col_ext, 'gx', axis=1, tiled=True)  33.5 us
  transfers between devices with their start and end apart: 34, of which 19 were waited for; matrix products, arithmetic and copies ran while one was open for 3% of the time, Pallas kernels for 0%

profile of v1, /device:TPU:4, one launch (start us, length us, event | category | flops | bytes accessed | tf_op | source)
XLA Modules:
  0.0 999.6 jit_solution(15304466553970694971)
XLA Ops:
  8.6 1.7 collective-permute-start
  10.4 1.3 collective-permute-start.1
  11.7 3.1 collective-permute-done.1
  14.8 3.1 collective-permute-start.2
  17.9 2.7 collective-permute-start.3
  20.9 2.6 collective-permute-done.3
  32.6 5.8 collective-permute-start.4
  38.5 1.9 collective-permute-start.5
  40.4 3.5 collective-permute-done.5
  44.0 33.5 %all_gather.3 = bf16[64,16,24]{0,2,1:T(8,128)(2,1)S(1)} all-gather(bf16[64,1,24]{0,2,1:T(8,128)(2,1)S(1)} %pad_maximum_fusion.21), channel_id=1, replica_groups=mesh['gx'=16,'gy'=16] {'gx'}, dimensions={1}, use_global_device_ids=true | all-gather | bytes 52224 | tf_op jit(solution)/shard_map/all_gather | solution.py:149
  84.5 6.4 all-to-all-start
  91.0 9.9 all-to-all-done
  101.2 2.0 collective-permute-start.6
  103.3 1.3 collective-permute-start.7
  104.6 1.9 collective-permute-done.7
  106.4 4.2 collective-permute-start.8
  110.6 1.9 collective-permute-start.9
  112.6 3.7 collective-permute-done.9
  116.9 1.3 copy-done.1
  124.2 3.1 collective-permute-start.10
  128.6 2.7 collective-permute-done.11
  131.5 4.1 collective-permute-start.12
  135.5 2.1 collective-permute-start.13
  137.7 3.6 collective-permute-done.13
  156.0 3.4 collective-permute-start.14
  163.9 4.1 collective-permute-start.16
  167.9 1.9 collective-permute-start.17
  171.3 2.8 collective-permute-done.17
  186.6 1.6 fusion.398
  188.3 1.6 fusion.400
  189.9 1.6 fusion.401
  191.5 1.6 fusion.403
  193.1 1.7 fusion.404
  194.8 1.6 fusion.406
  197.2 1.6 fusion.409
  202.6 1.6 fusion.418
  209.7 3.1 collective-permute-start.18
  212.8 1.5 collective-permute-start.19
  215.1 1.9 collective-permute-done.19
  217.2 4.0 collective-permute-start.20
  221.2 1.9 collective-permute-start.21
  223.9 3.5 collective-permute-done.21
  231.0 1.4 reshape.1158
  233.2 1.4 reshape.1160
  234.6 1.5 reshape.1161
  236.8 1.4 reshape.1163
  238.2 1.5 reshape.1164
  256.1 28.9 %all-to-all-start.1 = ((f32[16,1,128]{2,1,0:T(1,128)}), f32[16,1,128]{2,1,0:T(1,128)S(1)}, u32[]{:S(2)}, u32[]{:S(2)}) async-start(f32[16,1,128]{2,1,0:T(1,128)} %reshape.1246), calls=%async_computation.1 | async-start | bytes 16384 | tf_op jit(solution)/shard_map/all_to_all | solution.py:196
  285.9 9.1 all-to-all-done.1
  296.1 4.3 collective-permute-start.22
  300.4 1.9 collective-permute-start.23
  303.1 3.1 collective-permute-done.23
  317.9 67.3 %reduce-scatter.2.cloned.1.call-done = bf16[64,1,16]{0,2,1:T(8,128)(2,1)} async-done(((bf16[64,16,16]{0,2,1:T(8,128)(2,1)}), bf16[64,1,16]{0,2,1:T(8,128)(2,1)}) %reduce-scatter.2.cloned.1.call-update) | async-done | bytes 2064 | tf_op jit(solution)/shard_map/reduce_scatter | solution.py:206
  391.4 1.6 concatenate.78
  393.1 149.0 %all-reduce.15.cloned.1.call-done = f32[64,864]{0,1:T(8,128)} async-done(((f32[64,864]{0,1:T(8,128)}), f32[64,864]{0,1:T(8,128)}) %all-reduce.15.cloned.1.call-update) | async-done | bytes 221200 | tf_op jit(solution)/shard_map/psum | solution.py:213
  549.2 1.3 collective-permute-start.25
  550.5 3.2 collective-permute-done.25
  554.0 1.9 collective-permute-start.26
  555.9 5.5 collective-permute-start.27
  561.5 74.4 %psum.37 = bf16[8,1728]{1,0:T(8,128)(2,1)S(1)} all-reduce(bf16[8,1728]{1,0:T(8,128)(2,1)S(1)} %multiply_convert_fusion.3), channel_id=1, replica_groups=mesh['gx'=16,'gy'=16] {'gy'}, use_global_device_ids=true, to_apply=%region_7.8 | all-reduce | flops 13824 | bytes 55296 | tf_op jit(solution)/shard_map/psum | solution.py:209
  648.1 73.5 %all-reduce.17.cloned.1.call-done = f32[64,864]{0,1:T(8,128)} async-done(((f32[64,864]{0,1:T(8,128)}), f32[64,864]{0,1:T(8,128)}) %all-reduce.17.cloned.1.call-update) | async-done | bytes 221200 | tf_op jit(solution)/shard_map/psum | solution.py:213
  721.6 1.9 copy.98
  723.5 266.3 %all-reduce.19.cloned.1.call-done = (f32[64,5184]{1,0:T(8,128)}, f32[32,2592]{1,0:T(8,128)}) async-done(((f32[64,5184]{1,0:T(8,128)}, f32[32,2592]{1,0:T(8,128)}), (f32[64,5184]{1,0:T(8,128)}, f32[32,2592]{1,0:T(8,128)})) %all-reduce.19.cloned.1.call-update) | async-done | bytes 1658896 | tf_op jit(solution)/shard_map/psum | solution.py:186
  989.8 2.5 copy.160
  (910 shorter events, 130.7 us)
Async XLA Ops:
  8.6 3.1 collective-permute-start
  10.4 4.4 collective-permute-start.1
  11.7 104.6 %copy-start.123 = (pred[80]{0:T(512)(128)(4,1)}, pred[80]{0:T(512)(128)(4,1)S(1)}, u32[]{:S(2)}) copy-start(pred[80]{0:T(512)(128)(4,1)S(1)} %compare_and_fusion.4) | copy-start | bytes 244
  11.7 104.7 %copy-start.126 = (pred[80]{0:T(512)(128)(4,1)}, pred[80]{0:T(512)(128)(4,1)S(1)}, u32[]{:S(2)}) copy-start(pred[80]{0:T(512)(128)(4,1)S(1)} %compare_and_fusion.3) | copy-start | bytes 244
  14.8 6.0 collective-permute-start.2
  17.9 5.5 collective-permute-start.3
  20.7 95.7 %copy-start.129 = (pred[80]{0:T(512)(128)(4,1)}, pred[80]{0:T(512)(128)(4,1)S(1)}, u32[]{:S(2)}) copy-start(pred[80]{0:T(512)(128)(4,1)S(1)} %compare_and_fusion.6) | copy-start | bytes 244
  32.6 7.8 collective-permute-start.4
  38.5 5.5 collective-permute-start.5
  84.5 16.4 %all-to-all-start = ((bf16[8,16,16]{2,0,1:T(8,128)(2,1)}), bf16[8,16,16]{2,0,1:T(8,128)(2,1)S(1)}, u32[]{:S(2)}, u32[]{:S(2)}) async-start(bf16[8,16,16]{2,0,1:T(8,128)(2,1)} %copy.83), calls=%async_computation | async-start | bytes 65536 | tf_op jit(solution)/shard_map/all_to_all | solution.py:156
  101.2 3.3 collective-permute-start.6
  103.3 3.2 collective-permute-start.7
  106.4 6.1 collective-permute-start.8
  110.6 5.6 collective-permute-start.9
  124.2 4.5 collective-permute-start.10
  127.3 4.1 collective-permute-start.11
  131.5 6.2 collective-permute-start.12
  135.5 5.7 collective-permute-start.13
  156.0 6.4 collective-permute-start.14
  159.4 4.2 collective-permute-start.15
  163.9 7.4 collective-permute-start.16
  167.9 6.2 collective-permute-start.17
  209.7 5.4 collective-permute-start.18
  212.8 4.2 collective-permute-start.19
  217.2 6.7 collective-permute-start.20
  221.2 6.2 collective-permute-start.21
  256.1 38.8 %all-to-all-start.1 = ((f32[16,1,128]{2,1,0:T(1,128)}), f32[16,1,128]{2,1,0:T(1,128)S(1)}, u32[]{:S(2)}, u32[]{:S(2)}) async-start(f32[16,1,128]{2,1,0:T(1,128)} %reshape.1246), calls=%async_computation.1 | async-start | bytes 16384 | tf_op jit(solution)/shard_map/all_to_all | solution.py:196
  285.1 100.2 %reduce-scatter.2.cloned.1.call-start = ((), (), s32[]{:S(2)}) async-start(), calls=%async_computation.3 | async-start | bytes 69632 | tf_op jit(solution)/shard_map/reduce_scatter | solution.py:206
  296.1 7.0 collective-permute-start.22
  300.4 5.8 collective-permute-start.23
  312.6 73.8 %copy-start.67 = (bf16[32,128]{1,0:T(8,128)(2,1)S(1)}, bf16[32,128]{1,0:T(8,128)(2,1)}, u32[]{:S(2)}) copy-start(bf16[32,128]{1,0:T(8,128)(2,1)} %copy-done.66) | copy-start | bytes 24580
  312.8 73.8 %copy-start.71 = (bf16[32,128]{1,0:T(8,128)(2,1)S(1)}, bf16[32,128]{1,0:T(8,128)(2,1)}, u32[]{:S(2)}) copy-start(bf16[32,128]{1,0:T(8,128)(2,1)} %copy-done.70) | copy-start | bytes 24580
  312.8 73.9 %copy-start.73 = (bf16[32,128]{1,0:T(8,128)(2,1)S(1)}, bf16[32,128]{1,0:T(8,128)(2,1)}, u32[]{:S(2)}) copy-start(bf16[32,128]{1,0:T(8,128)(2,1)} %copy-done.72) | copy-start | bytes 24580
  313.1 73.8 %copy-start.75 = (bf16[32,128]{1,0:T(8,128)(2,1)S(1)}, bf16[32,128]{1,0:T(8,128)(2,1)}, u32[]{:S(2)}) copy-start(bf16[32,128]{1,0:T(8,128)(2,1)} %copy-done.74) | copy-start | bytes 24580
  313.1 73.9 %copy-start.77 = (bf16[32,128]{1,0:T(8,128)(2,1)S(1)}, bf16[32,128]{1,0:T(8,128)(2,1)}, u32[]{:S(2)}) copy-start(bf16[32,128]{1,0:T(8,128)(2,1)} %copy-done.76) | copy-start | bytes 24580
  313.1 74.0 %copy-start.79 = (bf16[32,128]{1,0:T(8,128)(2,1)S(1)}, bf16[32,128]{1,0:T(8,128)(2,1)}, u32[]{:S(2)}) copy-start(bf16[32,128]{1,0:T(8,128)(2,1)} %copy-done.78) | copy-start | bytes 24580
  313.1 74.2 %copy-start.81 = (bf16[32,128]{1,0:T(8,128)(2,1)S(1)}, bf16[32,128]{1,0:T(8,128)(2,1)}, u32[]{:S(2)}) copy-start(bf16[32,128]{1,0:T(8,128)(2,1)} %copy-done.80) | copy-start | bytes 24580
  313.3 74.1 %copy-start.83 = (bf16[32,128]{1,0:T(8,128)(2,1)S(1)}, bf16[32,128]{1,0:T(8,128)(2,1)}, u32[]{:S(2)}) copy-start(bf16[32,128]{1,0:T(8,128)(2,1)} %copy-done.82) | copy-start | bytes 24580
  313.3 74.2 %copy-start.85 = (bf16[32,128]{1,0:T(8,128)(2,1)S(1)}, bf16[32,128]{1,0:T(8,128)(2,1)}, u32[]{:S(2)}) copy-start(bf16[32,128]{1,0:T(8,128)(2,1)} %copy-done.84) | copy-start | bytes 24580
  313.3 74.4 %copy-start.87 = (bf16[32,128]{1,0:T(8,128)(2,1)S(1)}, bf16[32,128]{1,0:T(8,128)(2,1)}, u32[]{:S(2)}) copy-start(bf16[32,128]{1,0:T(8,128)(2,1)} %copy-done.86) | copy-start | bytes 24580
  313.6 74.2 %copy-start.89 = (bf16[32,128]{1,0:T(8,128)(2,1)S(1)}, bf16[32,128]{1,0:T(8,128)(2,1)}, u32[]{:S(2)}) copy-start(bf16[32,128]{1,0:T(8,128)(2,1)} %copy-done.88) | copy-start | bytes 24580
  313.6 74.3 %copy-start.91 = (bf16[32,128]{1,0:T(8,128)(2,1)S(1)}, bf16[32,128]{1,0:T(8,128)(2,1)}, u32[]{:S(2)}) copy-start(bf16[32,128]{1,0:T(8,128)(2,1)} %copy-done.90) | copy-start | bytes 24580
  313.6 74.5 %copy-start.93 = (bf16[32,128]{1,0:T(8,128)(2,1)S(1)}, bf16[32,128]{1,0:T(8,128)(2,1)}, u32[]{:S(2)}) copy-start(bf16[32,128]{1,0:T(8,128)(2,1)} %copy-done.92) | copy-start | bytes 24580
  313.7 74.6 %copy-start.95 = (bf16[32,128]{1,0:T(8,128)(2,1)S(1)}, bf16[32,128]{1,0:T(8,128)(2,1)}, u32[]{:S(2)}) copy-start(bf16[32,128]{1,0:T(8,128)(2,1)} %copy-done.94) | copy-start | bytes 24580
  313.9 74.5 %copy-start.97 = (bf16[32,128]{1,0:T(8,128)(2,1)S(1)}, bf16[32,128]{1,0:T(8,128)(2,1)}, u32[]{:S(2)}) copy-start(bf16[32,128]{1,0:T(8,128)(2,1)} %copy-done.96) | copy-start | bytes 24580
  313.9 74.6 %copy-start.99 = (bf16[32,128]{1,0:T(8,128)(2,1)S(1)}, bf16[32,128]{1,0:T(8,128)(2,1)}, u32[]{:S(2)}) copy-start(bf16[32,128]{1,0:T(8,128)(2,1)} %copy-done.98) | copy-start | bytes 24580
  313.9 74.8 %copy-start.101 = (bf16[32,128]{1,0:T(8,128)(2,1)S(1)}, bf16[32,128]{1,0:T(8,128)(2,1)}, u32[]{:S(2)}) copy-start(bf16[32,128]{1,0:T(8,128)(2,1)} %copy-done.100) | copy-start | bytes 24580
  314.2 74.6 %copy-start.103 = (bf16[32,128]{1,0:T(8,128)(2,1)S(1)}, bf16[32,128]{1,0:T(8,128)(2,1)}, u32[]{:S(2)}) copy-start(bf16[32,128]{1,0:T(8,128)(2,1)} %copy-done.102) | copy-start | bytes 24580
  314.2 74.7 %copy-start.105 = (bf16[32,128]{1,0:T(8,128)(2,1)S(1)}, bf16[32,128]{1,0:T(8,128)(2,1)}, u32[]{:S(2)}) copy-start(bf16[32,128]{1,0:T(8,128)(2,1)} %copy-done.104) | copy-start | bytes 24580
  314.2 74.9 %copy-start.107 = (bf16[32,128]{1,0:T(8,128)(2,1)S(1)}, bf16[32,128]{1,0:T(8,128)(2,1)}, u32[]{:S(2)}) copy-start(bf16[32,128]{1,0:T(8,128)(2,1)} %copy-done.106) | copy-start | bytes 24580
  314.4 74.8 %copy-start.109 = (bf16[32,128]{1,0:T(8,128)(2,1)S(1)}, bf16[32,128]{1,0:T(8,128)(2,1)}, u32[]{:S(2)}) copy-start(bf16[32,128]{1,0:T(8,128)(2,1)} %copy-done.108) | copy-start | bytes 24580
  314.4 74.9 %copy-start.111 = (bf16[32,128]{1,0:T(8,128)(2,1)S(1)}, bf16[32,128]{1,0:T(8,128)(2,1)}, u32[]{:S(2)}) copy-start(bf16[32,128]{1,0:T(8,128)(2,1)} %copy-done.110) | copy-start | bytes 24580
  314.4 75.1 %copy-start.113 = (bf16[32,128]{1,0:T(8,128)(2,1)S(1)}, bf16[32,128]{1,0:T(8,128)(2,1)}, u32[]{:S(2)}) copy-start(bf16[32,128]{1,0:T(8,128)(2,1)} %copy-done.112) | copy-start | bytes 24580
  314.4 75.2 %copy-start.121 = (bf16[32,128]{1,0:T(8,128)(2,1)S(1)}, bf16[32,128]{1,0:T(8,128)(2,1)}, u32[]{:S(2)}) copy-start(bf16[32,128]{1,0:T(8,128)(2,1)} %copy-done.120) | copy-start | bytes 24580
  317.1 225.0 %all-reduce.15.cloned.1.call-start = ((), (), s32[]{:S(2)}) async-start(), calls=%async_computation.4 | async-start | bytes 884736 | tf_op jit(solution)/shard_map/psum | solution.py:213
  390.6 331.0 %all-reduce.17.cloned.1.call-start = ((), (), s32[]{:S(2)}) async-start(), calls=%async_computation.5 | async-start | bytes 884736 | tf_op jit(solution)/shard_map/psum | solution.py:213
  542.1 447.7 %all-reduce.19.cloned.1.call-start = ((), (), s32[]{:S(2)}) async-start(), calls=%async_computation.6 | async-start | bytes 3375104 | tf_op jit(solution)/shard_map/psum | solution.py:186
  544.6 91.9 %copy-start.125 = (pred[80]{0:T(512)(128)(4,1)S(1)}, pred[80]{0:T(512)(128)(4,1)}, u32[]{:S(2)}) copy-start(pred[80]{0:T(512)(128)(4,1)} %copy-done.123) | copy-start | bytes 244
  545.2 91.6 %copy-start.128 = (pred[80]{0:T(512)(128)(4,1)S(1)}, pred[80]{0:T(512)(128)(4,1)}, u32[]{:S(2)}) copy-start(pred[80]{0:T(512)(128)(4,1)} %copy-done.126) | copy-start | bytes 244
  545.2 91.6 %copy-start.131 = (pred[80]{0:T(512)(128)(4,1)S(1)}, pred[80]{0:T(512)(128)(4,1)}, u32[]{:S(2)}) copy-start(pred[80]{0:T(512)(128)(4,1)} %copy-done.129) | copy-start | bytes 244
  547.9 2.6 collective-permute-start.24
  549.2 4.6 collective-permute-start.25
  554.0 82.5 %collective-permute-start.26 = (bf16[64,4,8]{2,1,0:T(4,128)(2,1)S(1)}, bf16[64,4,8]{2,1,0:T(4,128)(2,1)S(1)}, u32[]{:S(2)}, u32[]{:S(2)}) collective-permute-start(bf16[64,4,8]{2,1,0:T(4,128)(2,1)S(1)} %get-tuple-element.203), channel_id=1, source_target_pairs={{0,1},{1,2},{2,3},{3,4},{4,5},{5,6},{6,7},{7,8},{8,9},{9,10},{10,1... | collective-permute-start | bytes 12296 | tf_op jit(solution)/shard_map/ppermute | solution.py:18
  555.9 80.5 %collective-permute-start.27 = (bf16[64,4,8]{2,1,0:T(4,128)(2,1)S(1)}, bf16[64,4,8]{2,1,0:T(4,128)(2,1)S(1)}, u32[]{:S(2)}, u32[]{:S(2)}) collective-permute-start(bf16[64,4,8]{2,1,0:T(4,128)(2,1)S(1)} %get-tuple-element.204), channel_id=1, source_target_pairs={{1,0},{2,1},{3,2},{4,3},{5,4},{6,5},{7,6},{8,7},{9,8},{10,9},{11,1... | collective-permute-start | bytes 12296 | tf_op jit(solution)/shard_map/ppermute | solution.py:20
  (113 other events, 1710.1 us)
Sparse Core Ops, SparseCore 0:
  317.2 67.9 reduce-scatter.1
  390.7 151.3 all-reduce.14
  544.7 176.8 all-reduce.16
  727.5 262.2 all-reduce.18
